TPU v7x, 512 devices: a whole 4x4x16 slice. The times are simulated.
512 devices in a mesh: grp: 32 (over z, x_lo), ep: 16 (over y, x_hi, core).
Axes of the slice: x: 4 (x_hi: 2, x_lo: 2; x = x_hi * 2 + x_lo), y: 4, z: 16, core: 2. Of those that a mesh axis runs over, the one named last changes fastest.
Arguments:
- hidden: bfloat16 [256, 1536], P('grp', 'ep'), may hold values from -12 to 12
- query: bfloat16 [256, 1536], P('grp'), may hold values from -16 to 16
- new_kv: bfloat16 [256, 2, 512], P('grp'), may hold values from -4 to 4
- key_cache: bfloat16 [98304, 512], P(('grp', 'ep')), may hold values from -6 to 6
- value_cache: bfloat16 [98304, 512], P(('grp', 'ep')), may hold values from -4 to 4
- page_owner: int32 [6144], P(('grp', 'ep')), may hold values from 0 to 15, as said below
- page_fill: int32 [6144], P(('grp', 'ep')), may hold values from 1 to 16, as said below
- out_weight: bfloat16 [1536, 1536], P('grp', 'ep'), may hold values from -0.75 to 0.75
- norm_gain: float32 [1536], P('ep'), may hold values from 0.25 to 1.75
- gate_up: bfloat16 [32, 1536, 1024], P('grp'), may hold values from -0.15625 to 0.15625
- down: bfloat16 [32, 512, 1536], P('grp'), may hold values from -0.25 to 0.25
- routes: int32 [256, 8], P('grp'), may hold values from 0 to 31, all different within a row; in each aligned block of 8 rows (0 to 7, 8 to 15, ...) at most 4 rows name the same one
- route_weight: bfloat16 [256, 8], P('grp'), may hold values from 0.049804688 to 0.3984375
Outputs:
- layer_out: bfloat16 [256, 1536], P('grp', 'ep')
- attn_out: bfloat16 [256, 1536], P('grp')
Inputs may be any that keep to these rules, and one draw needn't show every extreme that they name: `routes`: each row names 8 different experts. In each group's 8 rows (aligned blocks of 8 rows) no expert is named by more than 4 rows, a bound that some block reaches. `page_owner`: A value r under 8 names row r of the page's own group; a value 8 + r names row r of the partner group, whose index differs in the lowest bit. The first page_fill[p] tokens of page p are cached; the rest of the page is unused. The first page of every device is full.
All inputs are finite; a program needn't handle non-finite values.
Results may differ from a plain program's by a relative error of at most 0.017.
Values may be sent and summed in bfloat16 or wider, within the bound.
A program may use at most 64 MiB of HBM per device.

v0:
```python
import jax
import jax.numpy as jnp
from jax import lax
from jax.sharding import PartitionSpec as P

D = 1536
HEADS = 24
KV_HEADS = 8
HD = 64
FF = 512
TOP = 8
masked_score = -1e30
norm_epsilon = 1e-05


def from_partner(block, axis, apart):
    count = lax.axis_size(axis)
    route = []
    for low in range(count):
        high = low | 1 << apart
        if high != low and high < count:
            route += [(low, high), (high, low)]
    return lax.ppermute(block, axis, route)


def combined_all(part, axis, combine):
    gathered = jax.tree.map(lambda a: lax.all_gather(a, axis), part)

    def take(source):
        return jax.tree.map(lambda a: lax.dynamic_index_in_dim(a, source, 0, False), gathered)

    return lax.fori_loop(
        1, lax.axis_size(axis), lambda source, state: combine(state, take(source)), take(0)
    )


def merge_parts(earlier, later):
    max_one, total_one, accum_one = earlier
    max_two, total_two, accum_two = later
    highest = jnp.maximum(max_one, max_two)
    factor_one = jnp.exp(max_one - highest)
    factor_two = jnp.exp(max_two - highest)
    return (
        highest,
        total_one * factor_one + total_two * factor_two,
        accum_one * factor_one[..., None] + accum_two * factor_two[..., None],
    )


def per_device(
    hidden,
    query,
    new_kv,
    key_cache,
    value_cache,
    page_owner,
    page_fill,
    out_weight,
    norm_gain,
    gate_up,
    down,
    routes,
    route_weight,
):
    row_count = query.shape[0]
    group_count = lax.axis_size("grp")
    head_group = HEADS // KV_HEADS
    page_count = page_owner.shape[0]
    token_count = key_cache.shape[0]
    page_length = token_count // page_count
    both_rows = 2 * row_count
    scale = HD ** (-0.5)
    partner_query = from_partner(query, "grp", 0)
    all_queries = jnp.concatenate([query, partner_query], 0)
    query_heads = (
        all_queries.reshape(both_rows, KV_HEADS, head_group, HD)
        .transpose(1, 0, 2, 3)
        .reshape(KV_HEADS, both_rows * head_group, HD)
    )
    key_heads = key_cache.reshape(token_count, KV_HEADS, HD)
    value_heads = value_cache.reshape(token_count, KV_HEADS, HD)
    scores = (
        jnp.einsum("kqd,tkd->kqt", query_heads, key_heads, preferred_element_type=jnp.float32)
        * scale
    )
    scores = scores.reshape(KV_HEADS, both_rows, head_group, token_count)
    row_index = jnp.arange(both_rows, dtype=jnp.int32)
    in_page = jnp.arange(page_length, dtype=jnp.int32)
    usable = (page_owner[None, :, None] == row_index[:, None, None]) & (
        in_page[None, None, :] < page_fill[None, :, None]
    )
    usable = usable.reshape(both_rows, token_count)[None, :, None, :]
    local_top = jnp.max(jnp.where(usable, scores, masked_score), -1)
    weights = jnp.where(usable, jnp.exp(scores - local_top[..., None]), 0.0)
    local_total = jnp.sum(weights, -1)
    rounded = weights.astype(jnp.bfloat16).reshape(KV_HEADS, both_rows * head_group, token_count)
    local_accum = jnp.einsum(
        "kqt,tkd->kqd", rounded, value_heads, preferred_element_type=jnp.float32
    )
    part_max = local_top.transpose(1, 0, 2).reshape(both_rows, HEADS)
    part_total = local_total.transpose(1, 0, 2).reshape(both_rows, HEADS)
    part_accum = (
        local_accum.reshape(KV_HEADS, both_rows, head_group, HD)
        .transpose(1, 0, 2, 3)
        .reshape(both_rows, HEADS, HD)
    )
    merged = combined_all((part_max, part_total, part_accum), "ep", merge_parts)
    returned = from_partner(
        (merged[0][row_count:], merged[1][row_count:], merged[2][row_count:]), "grp", 0
    )
    combined = merge_parts(
        (merged[0][:row_count], merged[1][:row_count], merged[2][:row_count]), returned
    )
    own_query = query.reshape(row_count, KV_HEADS, head_group, HD)
    fresh_key = new_kv[:, 0].reshape(row_count, KV_HEADS, HD)
    fresh_value = new_kv[:, 1].astype(jnp.float32).reshape(row_count, KV_HEADS, HD)
    own_score = (
        jnp.einsum(
            "rkgd,rkd->rkg", own_query, fresh_key, preferred_element_type=jnp.float32
        ).reshape(row_count, HEADS)
        * scale
    )
    cache_max, cache_total, cache_accum = combined
    highest = jnp.maximum(cache_max, own_score)
    cache_factor = jnp.exp(cache_max - highest)
    own_weight = jnp.exp(own_score - highest)
    value_rows = jnp.broadcast_to(
        fresh_value[:, :, None, :], (row_count, KV_HEADS, head_group, HD)
    ).reshape(row_count, HEADS, HD)
    numerator = cache_accum * cache_factor[..., None] + own_weight[..., None] * value_rows
    denominator = cache_total * cache_factor + own_weight
    attn_out = (
        (numerator / denominator[..., None]).reshape(row_count, HEADS * HD).astype(jnp.bfloat16)
    )
    head_share = out_weight.shape[0]
    feature_share = hidden.shape[1]
    every_head = lax.all_gather(attn_out, "grp", axis=0, tiled=True)
    head_columns = lax.dynamic_slice_in_dim(
        every_head, lax.axis_index("grp") * head_share, head_share, 1
    )
    projected = lax.psum_scatter(
        jnp.dot(head_columns, out_weight, preferred_element_type=jnp.float32).astype(jnp.bfloat16),
        "grp",
        scatter_dimension=0,
        tiled=True,
    ).astype(jnp.float32)
    mixed = hidden.astype(jnp.float32) + projected
    squares = lax.psum(jnp.sum(mixed * mixed, -1), "ep")
    normed = (mixed * lax.rsqrt(squares / D + norm_epsilon)[:, None] * norm_gain).astype(
        jnp.bfloat16
    )
    capacity = min(row_count, 2 * row_count * TOP // group_count)
    expert_ids = jnp.arange(group_count, dtype=jnp.int32)
    flat_routes = routes.reshape(-1)
    hits = (flat_routes[:, None] == expert_ids[None, :]).astype(jnp.int32)
    earlier_hits = jnp.cumsum(hits, 0) - hits
    position = jnp.sum(earlier_hits * hits, 1)
    slot_index = flat_routes * capacity + position
    slots_all = jnp.arange(group_count * capacity, dtype=jnp.int32)
    picker = jnp.any(
        slot_index.reshape(row_count, TOP)[None, :, :] == slots_all[:, None, None], 2
    ).astype(jnp.bfloat16)
    sender = (
        jnp.dot(picker, normed, preferred_element_type=jnp.float32)
        .astype(jnp.bfloat16)
        .reshape(group_count, capacity, feature_share)
    )
    arrived = lax.all_to_all(sender, "grp", split_axis=0, concat_axis=0, tiled=True)
    whole_rows = lax.all_to_all(
        arrived.reshape(group_count * capacity, feature_share),
        "ep",
        split_axis=0,
        concat_axis=1,
        tiled=True,
    )
    pre_sum = jnp.dot(whole_rows, gate_up[0], preferred_element_type=jnp.float32)
    activated = (jax.nn.silu(pre_sum[:, :FF]) * pre_sum[:, FF:]).astype(jnp.bfloat16)
    result = jnp.dot(activated, down[0], preferred_element_type=jnp.float32).astype(jnp.bfloat16)
    served = lax.all_to_all(result, "ep", split_axis=1, concat_axis=0, tiled=True).reshape(
        group_count, capacity, feature_share
    )
    returned_rows = lax.all_to_all(served, "grp", split_axis=0, concat_axis=0, tiled=True)
    gathered_rows = returned_rows.reshape(group_count * capacity, feature_share)[
        slot_index
    ].reshape(row_count, TOP, feature_share)
    expert_mix = jnp.sum(
        route_weight.astype(jnp.float32)[:, :, None] * gathered_rows.astype(jnp.float32), 1
    )
    layer_out = (mixed + expert_mix).astype(jnp.bfloat16)
    return (layer_out, attn_out)


def solution(mesh):
    placed = (
        P("grp", "ep"),
        P("grp", None),
        P("grp", None, None),
        P(("grp", "ep"), None),
        P(("grp", "ep"), None),
        P(("grp", "ep")),
        P(("grp", "ep")),
        P("grp", "ep"),
        P("ep"),
        P("grp", None, None),
        P("grp", None, None),
        P("grp", None),
        P("grp", None),
    )
    return jax.shard_map(
        per_device,
        mesh=mesh,
        in_specs=placed,
        out_specs=(P("grp", "ep"), P("grp", None)),
        check_vma=False,
    )
```

profile of v0, /device:TPU:1, one launch (start us, length us, event | category | flops | bytes accessed | tf_op | source)
XLA Modules:
  0.0 435.2 jit_solution(1514925168340241131)
XLA Ops:
  7.2 4.2 collective-permute-start
  13.3 1.8 copy.96
  15.1 1.8 copy.104
  21.1 1.5 reshape.181
  22.6 1.4 slice_reduce_fusion
  24.0 1.4 reshape.199
  25.3 1.7 fusion.43
  27.0 1.5 copy.120
  28.5 1.3 bitcast_multiply_fusion.3
  31.1 1.4 convert_reduce_fusion
  32.5 1.4 reshape.186
  33.9 1.4 copy.112
  36.5 1.3 fusion.21
  37.9 1.4 reduce_window_sum.11
  39.3 1.4 select_reduce_fusion.1
  46.7 25.4 %all_gather.13 = f32[16,16,24]{2,1,0:T(8,128)S(1)} all-gather(f32[1,16,24]{2,1,0:T(8,128)S(1)} %copy.103), channel_id=1, replica_groups=mesh['grp'=32,'ep'=16] {'ep'}, dimensions={0}, use_global_device_ids=true | all-gather | bytes 26112 | tf_op jit(solution)/shard_map/all_gather | solution.py:27
  72.1 22.3 %all_gather.12 = f32[16,16,24]{2,1,0:T(8,128)S(1)} all-gather(f32[1,16,24]{2,1,0:T(8,128)S(1)} %copy.100), channel_id=1, replica_groups=mesh['grp'=32,'ep'=16] {'ep'}, dimensions={0}, use_global_device_ids=true | all-gather | bytes 26112 | tf_op jit(solution)/shard_map/all_gather | solution.py:27
  96.0 28.2 %while.19 = (s32[]{:T(128)}, f32[16,24]{1,0:T(8,128)S(1)}, f32[16,24]{1,0:T(8,128)S(1)}, f32[16,24,64]{2,1,0:T(8,128)S(1)}, f32[16,16,24]{2,1,0:T(8,128)}, /*ind...) while((s32[]{:T(128)}, f32[16,24]{1,0:T(8,128)S(1)}, ...), condition=%wide.region_3.4_spmd, body=%wide.region_2.3_spmd.sunk | while | flops 76037 | bytes 310423 | solution.py:32
  124.3 3.6 collective-permute-start.1
  128.7 1.9 collective-permute-start.3
  132.6 3.4 collective-permute-start.2
  136.8 1.7 collective-permute-done.2
  138.8 55.3 %all_gather.15 = bf16[256,1536]{1,0:T(8,128)(2,1)S(1)} all-gather(bf16[8,1536]{1,0:T(8,128)(2,1)S(1)} %convert_element_type.62), channel_id=1, replica_groups=mesh['grp'=32,'ep'=16] {'grp'}, dimensions={0}, use_global_device_ids=true | all-gather | bytes 811008 | tf_op jit(solution)/shard_map/all_gather | solution.py:137
  194.3 91.1 %all-reduce = bf16[256,96]{1,0:T(8,128)(2,1)S(1)} all-reduce(bf16[256,96]{1,0:T(8,128)(2,1)S(1)} %convolution_convert_fusion.1), channel_id=2, replica_groups=mesh['grp'=32,'ep'=16] {'grp'}, use_global_device_ids=true, to_apply=%region_4.5.clone | all-reduce | flops 24576 | bytes 98304
  286.3 75.5 %psum.7 = f32[8]{0:T(128)S(1)} all-reduce(f32[8]{0:T(128)S(1)} %multiply_reduce_fusion), channel_id=1, replica_groups=mesh['grp'=32,'ep'=16] {'ep'}, use_global_device_ids=true, to_apply=%region_9.10 | all-reduce | flops 8 | bytes 64 | tf_op jit(solution)/shard_map/psum | solution.py:148
  362.9 21.1 %all_to_all.45 = bf16[32,4,96]{2,1,0:T(4,128)(2,1)} all-to-all(bf16[32,4,96]{2,1,0:T(4,128)(2,1)S(1)} %bitcast.92), channel_id=1, replica_groups=mesh['grp'=32,'ep'=16] {'grp'}, dimensions={0} | all-to-all | bytes 49152 | tf_op jit(solution)/shard_map/all_to_all | solution.py:168
  384.0 5.4 %all-to-all-start.1 = ((bf16[16,8,96]{2,1,0:T(8,128)(2,1)}), bf16[16,8,96]{2,1,0:T(8,128)(2,1)S(1)}, u32[]{:S(2)}, u32[]{:S(2)}) async-start(bf16[16,8,96]{2,1,0:T(8,128)(2,1)} %bitcast.18), calls=%async_computation.1 | async-start | bytes 65536 | tf_op jit(solution)/shard_map/all_to_all | solution.py:169
  389.4 7.3 %all-to-all-done.1 = bf16[16,8,96]{2,1,0:T(8,128)(2,1)S(1)} async-done(((bf16[16,8,96]{2,1,0:T(8,128)(2,1)}), bf16[16,8,96]{2,1,0:T(8,128)(2,1)S(1)}, u32[]{:S(2)}, u32[]{:S(2)}) %all-to-all-start.1) | async-done | bytes 24608 | tf_op jit(solution)/shard_map/all_to_all | solution.py:169
  399.3 4.2 all-to-all-start.2
  403.5 7.4 %all-to-all-done.2 = bf16[8,16,96]{2,0,1:T(8,128)(2,1)} async-done(((bf16[8,16,96]{2,0,1:T(8,128)(2,1)}), bf16[8,16,96]{2,0,1:T(8,128)(2,1)}, u32[]{:S(2)}, u32[]{:S(2)}) %all-to-all-start.2) | async-done | bytes 24608 | tf_op jit(solution)/shard_map/all_to_all | solution.py:179
  411.0 3.9 all-to-all-start.3
  414.8 12.2 %all-to-all-done.3 = bf16[32,4,96]{2,1,0:T(4,128)(2,1)S(1)} async-done(((bf16[32,4,96]{2,1,0:T(4,128)(2,1)}), bf16[32,4,96]{2,1,0:T(4,128)(2,1)S(1)}, u32[]{:S(2)}, u32[]{:S(2)}) %all-to-all-start.3) | async-done | bytes 24608 | tf_op jit(solution)/shard_map/all_to_all | solution.py:182
  (127 shorter events, 53.5 us)
Async XLA Ops:
  7.2 389.6 %copy-start = (bf16[1,1536,1024]{2,1,0:T(8,128)(2,1)S(1)}, bf16[1,1536,1024]{2,1,0:T(8,128)(2,1)}, u32[]{:S(2)}) copy-start(bf16[1,1536,1024]{2,1,0:T(8,128)(2,1)} %param.24) | copy-start | bytes 9437188
  7.2 87.8 %all-gather.2.cloned.1.call-start = ((), (), s32[]{:S(2)}) async-start(), calls=%async_computation.4 | async-start | bytes 3342336 | tf_op jit(solution)/shard_map/all_gather | solution.py:27
  7.2 9.6 %collective-permute-start = (bf16[8,1536]{1,0:T(8,128)(2,1)}, bf16[8,1536]{1,0:T(8,128)(2,1)S(1)}, u32[]{:S(2)}, u32[]{:S(2)}) collective-permute-start(bf16[8,1536]{1,0:T(8,128)(2,1)} %param.16), channel_id=1, source_target_pairs={{0,16},{16,0},{32,48},{48,32},{64,80},{80,64},{96,112},{112,96},{1... | collective-permute-start | bytes 73736 | tf_op jit(solution)/shard_map/ppermute | solution.py:23
  44.8 91.2 %copy-start.5 = (f32[8,24]{0,1:T(8,128)S(1)}, f32[8,24]{0,1:T(8,128)}, u32[]{:S(2)}) copy-start(f32[8,24]{0,1:T(8,128)} %mul.194) | copy-start | bytes 2308
  44.8 93.6 %copy-start.3 = (f32[8,8,64]{2,0,1:T(8,128)S(1)}, f32[8,8,64]{2,0,1:T(8,128)}, u32[]{:S(2)}) copy-start(f32[8,8,64]{2,0,1:T(8,128)} %copy.112) | copy-start | bytes 49156
  72.1 122.0 %copy-start.8 = (bf16[48,96]{1,0:T(8,128)(2,1)S(1)}, bf16[48,96]{1,0:T(8,128)(2,1)}, u32[]{:S(2)}) copy-start(bf16[48,96]{1,0:T(8,128)(2,1)} %param.22) | copy-start | bytes 27652
  94.4 0.6 copy-start.2
  95.0 191.1 %copy-start.6 = (s32[8,8]{1,0:T(8,128)S(1)}, s32[8,8]{1,0:T(8,128)}, u32[]{:S(2)}) copy-start(s32[8,8]{1,0:T(8,128)} %get-tuple-element.221) | copy-start | bytes 772
  96.0 293.4 %copy-start.7 = (s32[8,8]{1,0:T(8,128)S(1)}, s32[8,8]{1,0:T(8,128)}, u32[]{:S(2)}) copy-start(s32[8,8]{1,0:T(8,128)} %get-tuple-element.220) | copy-start | bytes 772
  124.3 11.7 %collective-permute-start.1 = (f32[8,24]{0,1:T(8,128)S(1)}, f32[8,24]{0,1:T(8,128)}, u32[]{:S(2)}, u32[]{:S(2)}) collective-permute-start(f32[8,24]{0,1:T(8,128)S(1)} %slice.47), channel_id=1, source_target_pairs={{0,16},{16,0},{32,48},{48,32},{64,80},{80,64},{96,112},{112,96},{1... | collective-permute-start | bytes 2312 | tf_op jit(solution)/shard_map/ppermute | solution.py:23
  128.7 7.3 %collective-permute-start.3 = (f32[8,24]{0,1:T(8,128)}, f32[8,24]{0,1:T(8,128)}, u32[]{:S(2)}, u32[]{:S(2)}) collective-permute-start(f32[8,24]{0,1:T(8,128)} %slice.50), channel_id=1, source_target_pairs={{0,16},{16,0},{32,48},{48,32},{64,80},{80,64},{96,112},{112,96},{1... | collective-permute-start | bytes 2312 | tf_op jit(solution)/shard_map/ppermute | solution.py:23
  132.6 5.8 %collective-permute-start.2 = (f32[8,24,64]{2,0,1:T(8,128)S(1)}, f32[8,24,64]{2,0,1:T(8,128)S(1)}, u32[]{:S(2)}, u32[]{:S(2)}) collective-permute-start(f32[8,24,64]{2,0,1:T(8,128)S(1)} %slice.48), channel_id=1, source_target_pairs={{0,16},{16,0},{32,48},{48,32},{64,80},{80,64},{96,112},{112,96},{1... | collective-permute-start | bytes 147464 | tf_op jit(solution)/shard_map/ppermute | solution.py:23
  138.8 259.8 %copy-start.4 = (bf16[8,1536]{1,0:T(8,128)(2,1)}, bf16[8,1536]{1,0:T(8,128)(2,1)S(1)}, u32[]{:S(2)}) copy-start(bf16[8,1536]{1,0:T(8,128)(2,1)S(1)} %convert_element_type.62) | copy-start | bytes 73732
  138.8 264.7 %copy-start.10 = (s32[64]{0:T(128)S(1)}, s32[64]{0:T(128)}, u32[]{:S(2)}) copy-start(s32[64]{0:T(128)} %select_reduce_fusion.1) | copy-start | bytes 772
  138.8 264.7 %copy-start.11 = (bf16[8,8]{1,0:T(8,128)(2,1)S(1)}, bf16[8,8]{1,0:T(8,128)(2,1)}, u32[]{:S(2)}) copy-start(bf16[8,8]{1,0:T(8,128)(2,1)} %param.27) | copy-start | bytes 388
  194.1 233.7 %copy-start.9 = (bf16[8,96]{1,0:T(8,128)(2,1)S(1)}, bf16[8,96]{1,0:T(8,128)(2,1)}, u32[]{:S(2)}) copy-start(bf16[8,96]{1,0:T(8,128)(2,1)} %param.15) | copy-start | bytes 4612
  384.0 12.7 %all-to-all-start.1 = ((bf16[16,8,96]{2,1,0:T(8,128)(2,1)}), bf16[16,8,96]{2,1,0:T(8,128)(2,1)S(1)}, u32[]{:S(2)}, u32[]{:S(2)}) async-start(bf16[16,8,96]{2,1,0:T(8,128)(2,1)} %bitcast.18), calls=%async_computation.1 | async-start | bytes 65536 | tf_op jit(solution)/shard_map/all_to_all | solution.py:169
  396.8 1.4 copy-start.1
  399.3 11.7 %all-to-all-start.2 = ((bf16[8,16,96]{2,0,1:T(8,128)(2,1)}), bf16[8,16,96]{2,0,1:T(8,128)(2,1)}, u32[]{:S(2)}, u32[]{:S(2)}) async-start(bf16[8,16,96]{2,0,1:T(8,128)(2,1)} %copy.118), calls=%async_computation.2 | async-start | bytes 65536 | tf_op jit(solution)/shard_map/all_to_all | solution.py:179
  411.0 16.1 %all-to-all-start.3 = ((bf16[32,4,96]{2,1,0:T(4,128)(2,1)}), bf16[32,4,96]{2,1,0:T(4,128)(2,1)S(1)}, u32[]{:S(2)}, u32[]{:S(2)}) async-start(bf16[32,4,96]{2,1,0:T(4,128)(2,1)} %bitcast.23), calls=%async_computation.3 | async-start | bytes 65536 | tf_op jit(solution)/shard_map/all_to_all | solution.py:182
Sparse Core Ops, SparseCore 0:
  21.2 71.9 all-gather.1
where the time goes:
time: 438 us; the launch traced here: 435 us
  blocking collectives  291 us (66%)
  other arithmetic  40.8 us (9%)
  waiting for transfers between devices  28.6 us (7%)
  local copies, waits for them, and re-layouts  27.1 us (6%)
  starting transfers between devices  26.6 us (6%)
  between operations  15 us (3%)
  matrix products  6.08 us (1%)
    unnamed x1, blocking collectives  91.1 us
    psum x1, blocking collectives, per_device(): squares = lax.psum(jnp.sum(mixed * mixed, -1), 'ep')  75.5 us
    all_gather x1, blocking collectives, per_device(): every_head = lax.all_gather(attn_out, 'grp', axis=0, tiled=True)  55.3 us
    all_gather x2, blocking collectives, combined_all(): gathered = jax.tree.map(lambda a: lax.all_gather(a, axis), part)  47.7 us
    all_to_all x1, blocking collectives, per_device(): lax.all_to_all(sender, 'grp', split_axis=0, concat_axis=0, tiled=True)  21.1 us
    add x15, other arithmetic, merge_parts(): accum_one * factor_one[..., None] + accum_two * factor_two[..., None]  17 us
    ppermute x4, starting transfers between devices, from_partner(): return lax.ppermute(block, axis, route)  13.1 us
    all_to_all x1, waiting for transfers between devices, per_device(): lax.all_to_all(served, 'grp', split_axis=0, concat_axis=0, tiled=True)  12.2 us
  transfers between devices with their start and end apart: 8, of which 4 were waited for; matrix products, arithmetic and copies ran while one was open for 8% of the time, Pallas kernels for 0%

commit v1 on v0

--- a/solution.py
+++ b/solution.py
@@ -134,7 +134,9 @@
     )
     head_share = out_weight.shape[0]
     feature_share = hidden.shape[1]
-    every_head = lax.all_gather(attn_out, "grp", axis=0, tiled=True)
+    every_head = jnp.concatenate(
+        lax.all_to_all(jnp.stack([attn_out] * lax.axis_size("grp")), "grp", 0, 0), axis=0
+    )
     head_columns = lax.dynamic_slice_in_dim(
         every_head, lax.axis_index("grp") * head_share, head_share, 1
     )

time: 438 us -> 416 us (0.950)
  blocking collectives: 291 us -> 219 us
  waiting for transfers between devices: 28.6 us -> 80.4 us
  starting transfers between devices: 26.6 us -> 38 us
  other arithmetic: 40.8 us -> 32.9 us
  local copies, waits for them, and re-layouts: 27.1 us -> 21.1 us
    all_gather x1 -> x0, blocking collectives: 55.3 us -> none  [per_device(): every_head = lax.all_gather(attn_out, 'grp', axis=0, tiled=True)]
    all_to_all x0 -> x1, waiting for transfers between devices: none -> 39.1 us  [per_device(): lax.all_to_all(jnp.stack([attn_out] * lax.axis_size('grp')), 'grp', 0, 0)]
    all_to_all x0 -> x1, starting transfers between devices: none -> 12.8 us  [per_device(): lax.all_to_all(jnp.stack([attn_out] * lax.axis_size('grp')), 'grp', 0, 0)]
    all_gather x1, waiting for transfers between devices: 0.01 us -> 11.2 us  [combined_all(): gathered = jax.tree.map(lambda a: lax.all_gather(a, axis), part)]
    psum x1, blocking collectives: 75.5 us -> 64.7 us  [per_device(): squares = lax.psum(jnp.sum(mixed * mixed, -1), 'ep')]
    all_to_all x1, blocking collectives: 21.1 us -> 16.1 us  [per_device(): lax.all_to_all(sender, 'grp', split_axis=0, concat_axis=0, tiled=True)]
  transfers between devices with their start and end apart: 8 -> 9, of which waited for: 4 -> 6; matrix products, arithmetic and copies ran while one was open for 8% -> 5% of each run, Pallas kernels for 0% -> 0%
where the time goes in v1:
time: 416 us; the launch traced here: 413 us
  blocking collectives  219 us (53%)
  waiting for transfers between devices  80.4 us (19%)
  starting transfers between devices  38 us (9%)
  other arithmetic  32.9 us (8%)
  local copies, waits for them, and re-layouts  21.1 us (5%)
  between operations  15.1 us (4%)
  matrix products  6.28 us (2%)
    unnamed x1, blocking collectives  91.1 us
    psum x1, blocking collectives, per_device(): squares = lax.psum(jnp.sum(mixed * mixed, -1), 'ep')  64.7 us
    all_gather x2, blocking collectives, combined_all(): gathered = jax.tree.map(lambda a: lax.all_gather(a, axis), part)  47.3 us
    all_to_all x1, waiting for transfers between devices, per_device(): lax.all_to_all(jnp.stack([attn_out] * lax.axis_size('grp')), 'grp', 0, 0)  39.1 us
    add x15, other arithmetic, merge_parts(): accum_one * factor_one[..., None] + accum_two * factor_two[..., None]  17 us
    all_to_all x1, blocking collectives, per_device(): lax.all_to_all(sender, 'grp', split_axis=0, concat_axis=0, tiled=True)  16.1 us
    all_to_all x1, starting transfers between devices, per_device(): lax.all_to_all(jnp.stack([attn_out] * lax.axis_size('grp')), 'grp', 0, 0)  12.8 us
    all_to_all x1, waiting for transfers between devices, per_device(): lax.all_to_all(served, 'grp', split_axis=0, concat_axis=0, tiled=True)  12.2 us
  transfers between devices with their start and end apart: 9, of which 6 were waited for; matrix products, arithmetic and copies ran while one was open for 5% of the time, Pallas kernels for 0%

profile of v1, /device:TPU:1, one launch (start us, length us, event | category | flops | bytes accessed | tf_op | source)
XLA Modules:
  0.0 413.3 jit_solution(9160027082870541531)
XLA Ops:
  7.2 4.2 %collective-permute-start = (bf16[8,1536]{1,0:T(8,128)(2,1)}, bf16[8,1536]{1,0:T(8,128)(2,1)S(1)}, u32[]{:S(2)}, u32[]{:S(2)}) collective-permute-start(bf16[8,1536]{1,0:T(8,128)(2,1)} %param.16), channel_id=1, source_target_pairs={{0,16},{16,0},{32,48},{48,32},{64,80},{80,64},{96,112},{112,96},{1... | collective-permute-start | bytes 73736 | tf_op jit(solution)/shard_map/ppermute | solution.py:23
  13.3 1.8 copy.96
  15.1 1.8 copy.104
  17.8 1.2 select_reduce_fusion
  19.0 1.2 fusion.8
  21.1 1.5 reshape.187
  22.6 1.4 slice_reduce_fusion
  24.0 1.4 reshape.206
  25.3 1.7 fusion.43
  27.0 1.5 copy.120
  28.5 1.3 bitcast_multiply_fusion.3
  33.2 25.6 %all_gather.10 = f32[16,16,24]{2,1,0:T(8,128)S(1)} all-gather(f32[1,16,24]{2,1,0:T(8,128)S(1)} %copy.103), channel_id=1, replica_groups=mesh['grp'=32,'ep'=16] {'ep'}, dimensions={0}, use_global_device_ids=true | all-gather | bytes 26112 | tf_op jit(solution)/shard_map/all_gather | solution.py:27
  58.8 21.7 %all_gather.9 = f32[16,16,24]{2,1,0:T(8,128)S(1)} all-gather(f32[1,16,24]{2,1,0:T(8,128)S(1)} %copy.100), channel_id=1, replica_groups=mesh['grp'=32,'ep'=16] {'ep'}, dimensions={0}, use_global_device_ids=true | all-gather | bytes 26112 | tf_op jit(solution)/shard_map/all_gather | solution.py:27
  81.1 11.2 %all-gather.2.cloned.1.call-done = f32[16,16,24,64]{3,2,1,0:T(8,128)} async-done(((f32[1,16,24,64]{3,2,1,0:T(8,128)}), f32[16,16,24,64]{3,2,1,0:T(8,128)}) %all-gather.2.cloned.1.call-update) | async-done | bytes 1572880 | tf_op jit(solution)/shard_map/all_gather | solution.py:27
  93.3 28.1 %while.19 = (s32[]{:T(128)}, f32[16,24]{1,0:T(8,128)S(1)}, f32[16,24]{1,0:T(8,128)S(1)}, f32[16,24,64]{2,1,0:T(8,128)S(1)}, f32[16,16,24]{2,1,0:T(8,128)}, /*ind...) while((s32[]{:T(128)}, f32[16,24]{1,0:T(8,128)S(1)}, ...), condition=%wide.region_3.4_spmd, body=%wide.region_2.3_spmd.sunk | while | flops 76037 | bytes 310423 | solution.py:32
  95.9 1.1 fusion.54
  121.6 2.2 collective-permute-start.1
  123.9 3.1 collective-permute-start.3
  127.3 2.2 collective-permute-start.2
  129.5 3.1 collective-permute-done.2
  133.9 12.8 %all-to-all-start = ((bf16[32,8,1536]{2,1,0:T(8,128)(2,1)}), bf16[32,8,1536]{2,1,0:T(8,128)(2,1)}, u32[]{:S(2)}, u32[]{:S(2)}) async-start(bf16[32,8,1536]{2,1,0:T(8,128)(2,1)} %stack.2), calls=%async_computation | async-start | bytes 1572864 | tf_op jit(solution)/shard_map/all_to_all | solution.py:138
  147.3 1.3 dynamic-slice
  149.3 39.1 %all-to-all-done = bf16[32,8,1536]{2,1,0:T(8,128)(2,1)} async-done(((bf16[32,8,1536]{2,1,0:T(8,128)(2,1)}), bf16[32,8,1536]{2,1,0:T(8,128)(2,1)}, u32[]{:S(2)}, u32[]{:S(2)}) %all-to-all-start) | async-done | bytes 786464 | tf_op jit(solution)/shard_map/all_to_all | solution.py:138
  189.5 91.1 %all-reduce = bf16[256,96]{1,0:T(8,128)(2,1)S(1)} all-reduce(bf16[256,96]{1,0:T(8,128)(2,1)S(1)} %convolution_convert_fusion.1), channel_id=2, replica_groups=mesh['grp'=32,'ep'=16] {'grp'}, use_global_device_ids=true, to_apply=%region_4.5.clone | all-reduce | flops 24576 | bytes 98304
  280.8 64.7 %psum.7 = f32[8]{0:T(128)S(1)} all-reduce(f32[8]{0:T(128)S(1)} %multiply_reduce_fusion), channel_id=1, replica_groups=mesh['grp'=32,'ep'=16] {'ep'}, use_global_device_ids=true, to_apply=%region_9.10 | all-reduce | flops 8 | bytes 64 | tf_op jit(solution)/shard_map/psum | solution.py:150
  345.9 16.1 %all_to_all.50 = bf16[32,4,96]{2,1,0:T(4,128)(2,1)} all-to-all(bf16[32,4,96]{2,1,0:T(4,128)(2,1)S(1)} %bitcast.93), channel_id=1, replica_groups=mesh['grp'=32,'ep'=16] {'grp'}, dimensions={0} | all-to-all | bytes 49152 | tf_op jit(solution)/shard_map/all_to_all | solution.py:170
  362.1 5.4 %all-to-all-start.2 = ((bf16[16,8,96]{2,1,0:T(8,128)(2,1)}), bf16[16,8,96]{2,1,0:T(8,128)(2,1)S(1)}, u32[]{:S(2)}, u32[]{:S(2)}) async-start(bf16[16,8,96]{2,1,0:T(8,128)(2,1)} %bitcast.19), calls=%async_computation.2 | async-start | bytes 65536 | tf_op jit(solution)/shard_map/all_to_all | solution.py:171
  367.5 7.3 %all-to-all-done.2 = bf16[16,8,96]{2,1,0:T(8,128)(2,1)S(1)} async-done(((bf16[16,8,96]{2,1,0:T(8,128)(2,1)}), bf16[16,8,96]{2,1,0:T(8,128)(2,1)S(1)}, u32[]{:S(2)}, u32[]{:S(2)}) %all-to-all-start.2) | async-done | bytes 24608 | tf_op jit(solution)/shard_map/all_to_all | solution.py:171
  377.4 4.2 %all-to-all-start.3 = ((bf16[8,16,96]{2,0,1:T(8,128)(2,1)}), bf16[8,16,96]{2,0,1:T(8,128)(2,1)}, u32[]{:S(2)}, u32[]{:S(2)}) async-start(bf16[8,16,96]{2,0,1:T(8,128)(2,1)} %copy.118), calls=%async_computation.3 | async-start | bytes 65536 | tf_op jit(solution)/shard_map/all_to_all | solution.py:181
  381.6 7.4 %all-to-all-done.3 = bf16[8,16,96]{2,0,1:T(8,128)(2,1)} async-done(((bf16[8,16,96]{2,0,1:T(8,128)(2,1)}), bf16[8,16,96]{2,0,1:T(8,128)(2,1)}, u32[]{:S(2)}, u32[]{:S(2)}) %all-to-all-start.3) | async-done | bytes 24608 | tf_op jit(solution)/shard_map/all_to_all | solution.py:181
  389.1 3.9 all-to-all-start.4
  393.0 12.2 %all-to-all-done.4 = bf16[32,4,96]{2,1,0:T(4,128)(2,1)S(1)} async-done(((bf16[32,4,96]{2,1,0:T(4,128)(2,1)}), bf16[32,4,96]{2,1,0:T(4,128)(2,1)S(1)}, u32[]{:S(2)}, u32[]{:S(2)}) %all-to-all-start.4) | async-done | bytes 24608 | tf_op jit(solution)/shard_map/all_to_all | solution.py:184
  (127 shorter events, 43.3 us)
Async XLA Ops:
  7.2 367.8 %copy-start = (bf16[1,1536,1024]{2,1,0:T(8,128)(2,1)S(1)}, bf16[1,1536,1024]{2,1,0:T(8,128)(2,1)}, u32[]{:S(2)}) copy-start(bf16[1,1536,1024]{2,1,0:T(8,128)(2,1)} %param.24) | copy-start | bytes 9437188
  7.2 85.1 %all-gather.2.cloned.1.call-start = ((), (), s32[]{:S(2)}) async-start(), calls=%async_computation.5 | async-start | bytes 3342336 | tf_op jit(solution)/shard_map/all_gather | solution.py:27
  7.2 9.6 %collective-permute-start = (bf16[8,1536]{1,0:T(8,128)(2,1)}, bf16[8,1536]{1,0:T(8,128)(2,1)S(1)}, u32[]{:S(2)}, u32[]{:S(2)}) collective-permute-start(bf16[8,1536]{1,0:T(8,128)(2,1)} %param.16), channel_id=1, source_target_pairs={{0,16},{16,0},{32,48},{48,32},{64,80},{80,64},{96,112},{112,96},{1... | collective-permute-start | bytes 73736 | tf_op jit(solution)/shard_map/ppermute | solution.py:23
  31.3 95.7 %copy-start.5 = (bf16[8,2,512]{2,1,0:T(2,128)(2,1)S(1)}, bf16[8,2,512]{2,1,0:T(2,128)(2,1)}, u32[]{:S(2)}) copy-start(bf16[8,2,512]{2,1,0:T(2,128)(2,1)} %param.17) | copy-start | bytes 49156
  31.3 95.8 %copy-start.4 = (f32[8,8,3]{0,2,1:T(4,128)S(1)}, f32[8,8,3]{0,2,1:T(4,128)}, u32[]{:S(2)}) copy-start(f32[8,8,3]{0,2,1:T(4,128)} %bitcast_multiply_fusion.3) | copy-start | bytes 2308
  80.5 0.6 copy-start.2
  93.2 53.6 %copy-start.6 = (s32[8,8]{1,0:T(8,128)S(1)}, s32[8,8]{1,0:T(8,128)}, u32[]{:S(2)}) copy-start(s32[8,8]{1,0:T(8,128)} %param.26) | copy-start | bytes 772
  93.3 95.1 %copy-start.7 = (bf16[48,96]{1,0:T(8,128)(2,1)S(1)}, bf16[48,96]{1,0:T(8,128)(2,1)}, u32[]{:S(2)}) copy-start(bf16[48,96]{1,0:T(8,128)(2,1)} %param.22) | copy-start | bytes 27652
  93.3 187.3 %copy-start.8 = (bf16[8,96]{1,0:T(8,128)(2,1)S(1)}, bf16[8,96]{1,0:T(8,128)(2,1)}, u32[]{:S(2)}) copy-start(bf16[8,96]{1,0:T(8,128)(2,1)} %param.15) | copy-start | bytes 4612
  93.3 252.3 %copy-start.10 = (f32[96]{0:T(128)S(1)}, f32[96]{0:T(128)}, u32[]{:S(2)}) copy-start(f32[96]{0:T(128)} %param.23) | copy-start | bytes 1156
  121.6 7.9 %collective-permute-start.1 = (f32[8,24]{0,1:T(8,128)S(1)}, f32[8,24]{0,1:T(8,128)S(1)}, u32[]{:S(2)}, u32[]{:S(2)}) collective-permute-start(f32[8,24]{0,1:T(8,128)S(1)} %slice.47), channel_id=1, source_target_pairs={{0,16},{16,0},{32,48},{48,32},{64,80},{80,64},{96,112},{112,96},{1... | collective-permute-start | bytes 2312 | tf_op jit(solution)/shard_map/ppermute | solution.py:23
  123.9 5.5 %collective-permute-start.3 = (f32[8,24]{0,1:T(8,128)S(1)}, f32[8,24]{0,1:T(8,128)S(1)}, u32[]{:S(2)}, u32[]{:S(2)}) collective-permute-start(f32[8,24]{0,1:T(8,128)S(1)} %slice.50), channel_id=1, source_target_pairs={{0,16},{16,0},{32,48},{48,32},{64,80},{80,64},{96,112},{112,96},{1... | collective-permute-start | bytes 2312 | tf_op jit(solution)/shard_map/ppermute | solution.py:23
  127.3 5.4 %collective-permute-start.2 = (f32[8,24,64]{2,0,1:T(8,128)S(1)}, f32[8,24,64]{2,0,1:T(8,128)S(1)}, u32[]{:S(2)}, u32[]{:S(2)}) collective-permute-start(f32[8,24,64]{2,0,1:T(8,128)S(1)} %slice.48), channel_id=1, source_target_pairs={{0,16},{16,0},{32,48},{48,32},{64,80},{80,64},{96,112},{112,96},{1... | collective-permute-start | bytes 147464 | tf_op jit(solution)/shard_map/ppermute | solution.py:23
  132.9 242.5 %copy-start.3 = (bf16[8,1536]{1,0:T(8,128)(2,1)}, bf16[8,1536]{1,0:T(8,128)(2,1)S(1)}, u32[]{:S(2)}) copy-start(bf16[8,1536]{1,0:T(8,128)(2,1)S(1)} %convert_element_type.64) | copy-start | bytes 73732
  133.9 54.5 %all-to-all-start = ((bf16[32,8,1536]{2,1,0:T(8,128)(2,1)}), bf16[32,8,1536]{2,1,0:T(8,128)(2,1)}, u32[]{:S(2)}, u32[]{:S(2)}) async-start(bf16[32,8,1536]{2,1,0:T(8,128)(2,1)} %stack.2), calls=%async_computation | async-start | bytes 1572864 | tf_op jit(solution)/shard_map/all_to_all | solution.py:138
  146.8 234.9 %copy-start.9 = (bf16[8,8]{1,0:T(8,128)(2,1)S(1)}, bf16[8,8]{1,0:T(8,128)(2,1)}, u32[]{:S(2)}) copy-start(bf16[8,8]{1,0:T(8,128)(2,1)} %param.27) | copy-start | bytes 388
  362.1 12.7 %all-to-all-start.2 = ((bf16[16,8,96]{2,1,0:T(8,128)(2,1)}), bf16[16,8,96]{2,1,0:T(8,128)(2,1)S(1)}, u32[]{:S(2)}, u32[]{:S(2)}) async-start(bf16[16,8,96]{2,1,0:T(8,128)(2,1)} %bitcast.19), calls=%async_computation.2 | async-start | bytes 65536 | tf_op jit(solution)/shard_map/all_to_all | solution.py:171
  374.9 1.4 copy-start.1
  377.4 11.7 %all-to-all-start.3 = ((bf16[8,16,96]{2,0,1:T(8,128)(2,1)}), bf16[8,16,96]{2,0,1:T(8,128)(2,1)}, u32[]{:S(2)}, u32[]{:S(2)}) async-start(bf16[8,16,96]{2,0,1:T(8,128)(2,1)} %copy.118), calls=%async_computation.3 | async-start | bytes 65536 | tf_op jit(solution)/shard_map/all_to_all | solution.py:181
  389.1 16.1 %all-to-all-start.4 = ((bf16[32,4,96]{2,1,0:T(4,128)(2,1)}), bf16[32,4,96]{2,1,0:T(4,128)(2,1)S(1)}, u32[]{:S(2)}, u32[]{:S(2)}) async-start(bf16[32,4,96]{2,1,0:T(4,128)(2,1)} %bitcast.24), calls=%async_computation.4 | async-start | bytes 65536 | tf_op jit(solution)/shard_map/all_to_all | solution.py:184
Sparse Core Ops, SparseCore 0:
  21.2 71.0 all-gather.1
